TPU v7x, 32 devices: a whole 2x2x4 slice. The times are simulated.
32 devices in a mesh: groups: 2 (over x), section: 8 (over z, y), sub: 2 (over core).
Axes of the slice: x: 2, y: 2, z: 4, core: 2. Of those that a mesh axis runs over, the one named last changes fastest.
Arguments:
- voltages: bfloat16 [2048, 2, 65920], P(('groups', 'section', 'sub')), parts along dimension 0, may hold values from -6 to 6
- prototype: float32 [512], replicated, may hold values from 0.02 to 0.07
- beam_weights: bfloat16 [256, 2, 1024, 1024], P(('groups', 'section', 'sub')), parts along dimension 0, may hold values from -0.125 to 0.125
- input_order: int32 [1024], replicated, may hold values from 0 to 1023, each once
- beam_order: int32 [1024], replicated, may hold values from 0 to 1023, each once
- trial_delays: int32 [256, 128], replicated, may hold values from 0 to 127, as said below
Outputs:
- dedispersed: float32 [256, 2048, 128], P(None, ('groups', 'section', 'sub')), parts along dimension 1
There are 2 independent parts, one for each index of `groups`. A program takes and returns all parts, laid end to end along the dimension named above; an argument that names none is the same for every part. Nothing has to cross between parts.
Inputs may be any that keep to these rules, and one draw needn't show every extreme that they name: `input_order`: each physical input appears once. `beam_order`: each physical beam appears once. `trial_delays`: for each trial the delays do not rise with the channel index.
All inputs are finite; a program needn't handle non-finite values.
Results may differ from a plain program's by a relative error of at most 0.0043.
Values may be sent and summed in bfloat16 or wider, within the bound.
No kernel may reach another device: no remote copies, remote signals or barrier semaphores. Data moves between devices by JAX's collectives and lax.ppermute only.
A program may use at most 256 MiB of HBM per device.

v0:
```python
import math

import jax
import jax.numpy as jnp
from jax import lax
from jax.sharding import PartitionSpec as P

CHANS = 128
INPUTS = 1024
BEAMS = 1024
TAPS = 4
DOWN = 4
SPECTRA = 512
BINS = 128


def filter_matrix(prototype):
    channel_index = jnp.arange(CHANS, dtype=jnp.int32)
    phase_step = channel_index[:, None] * channel_index[None, :] % CHANS
    angles = 2.0 * math.pi / CHANS * phase_step.astype(jnp.float32)
    cosine = jnp.tile(jnp.cos(angles), (1, TAPS)) * prototype[None, :]
    sine_part = jnp.tile(jnp.sin(angles), (1, TAPS)) * prototype[None, :]
    real_rows = jnp.concatenate([cosine, sine_part], axis=1)
    imag_rows = jnp.concatenate([-sine_part, cosine], axis=1)
    return jnp.stack([real_rows, imag_rows], axis=0).astype(jnp.bfloat16)


def channelize(block_volts, matrix):
    input_count = block_volts.shape[0]
    frames = block_volts.reshape(input_count, 2, SPECTRA + TAPS - 1, CHANS)
    windows = jnp.concatenate(
        [
            frames[:, part_index, tap_index : tap_index + SPECTRA, :]
            for part_index in range(2)
            for tap_index in range(TAPS)
        ],
        axis=2,
    )
    result = lax.dot_general(
        matrix, windows, (((2,), (2,)), ((), ())), preferred_element_type=jnp.float32
    )
    return result.astype(jnp.bfloat16)


def fold_time(series):
    shape_head = series.shape[:-1]
    return series.reshape(shape_head + (series.shape[-1] // DOWN, DOWN)).sum(axis=-1)


def shards(voltages, prototype, beam_weights, input_order, beam_order, trial_delays):
    section_count = lax.axis_size("section")
    sub_count = lax.axis_size("sub")
    owners = section_count * sub_count
    chan_dev = CHANS // owners
    beam_dev = BEAMS // owners
    input_rows = jnp.arange(INPUTS, dtype=jnp.int32)
    channel_rows = jnp.arange(CHANS, dtype=jnp.int32)
    spectra_local = channelize(voltages, filter_matrix(prototype))
    physical = jnp.take(input_order, input_rows)
    position_of = (
        jnp.zeros((INPUTS,), jnp.int32).at[physical].set(jnp.arange(INPUTS, dtype=jnp.int32))
    )
    weight_real = beam_weights[:, 0]
    weight_imag = beam_weights[:, 1]
    ordered = jnp.take(
        lax.all_to_all(spectra_local, ("section", "sub"), split_axis=1, concat_axis=2, tiled=True),
        position_of,
        axis=2,
    )
    with_real = jnp.einsum(
        "cbi,pcit->pcbt", weight_real, ordered, preferred_element_type=jnp.float32
    )
    with_imag = jnp.einsum(
        "cbi,pcit->pcbt", weight_imag, ordered, preferred_element_type=jnp.float32
    )
    beam_real = with_real[0] - with_imag[1]
    beam_imag = with_real[1] + with_imag[0]
    power = beam_real * beam_real + beam_imag * beam_imag
    power = jnp.take(power, beam_order, axis=1)
    outgoing = fold_time(power)
    outgoing = outgoing.reshape(chan_dev, owners, beam_dev, outgoing.shape[2])
    half = BINS // 2 + 1
    delay_table = jnp.transpose(jnp.take(trial_delays, channel_rows, axis=1))
    sample_index = jnp.arange(BINS, dtype=jnp.int32)
    freq_index = jnp.arange(half, dtype=jnp.int32)
    half_angles = (
        2.0
        * math.pi
        / BINS
        * (freq_index[:, None] * sample_index[None, :] % BINS).astype(jnp.float32)
    )
    forward_cos = jnp.cos(half_angles)
    forward_sin = -jnp.sin(half_angles)
    edge = (freq_index == 0) | (freq_index == BINS // 2)
    fold_weight = (jnp.where(edge, 1.0, 2.0) / BINS).astype(jnp.float32)[:, None]
    inverse_cos = fold_weight * forward_cos
    inverse_sin = fold_weight * forward_sin
    twiddle_angles = (
        2.0
        * math.pi
        / BINS
        * (sample_index[:, None] * freq_index[None, :] % BINS).astype(jnp.float32)
    )
    twiddle = jnp.concatenate([jnp.cos(twiddle_angles), jnp.sin(twiddle_angles)], axis=1)
    twiddle_high = twiddle.astype(jnp.bfloat16)
    twiddle_low = (twiddle - twiddle_high.astype(jnp.float32)).astype(jnp.bfloat16)
    one_hot = (delay_table[:, :, None] == sample_index[None, None, :]).astype(jnp.bfloat16)
    phase_grid = jnp.einsum(
        "cdv,vf->cdf", one_hot, twiddle_high, preferred_element_type=jnp.float32
    ) + jnp.einsum("cdv,vf->cdf", one_hot, twiddle_low, preferred_element_type=jnp.float32)
    cos_grid = phase_grid[:, :, :half]
    sin_grid = phase_grid[:, :, half:]
    highest = lax.Precision.HIGHEST
    series = lax.all_to_all(outgoing, ("section", "sub"), split_axis=1, concat_axis=0, tiled=True)[
        :, 0
    ]
    centred = series - jnp.mean(series, axis=2, keepdims=True)
    spread = jnp.mean(centred * centred, axis=2, keepdims=True)
    normed = centred / jnp.sqrt(spread + 1e-06)
    spec_real = jnp.einsum("cbu,fu->fbc", normed, forward_cos, precision=highest)
    spec_imag = jnp.einsum("cbu,fu->fbc", normed, forward_sin, precision=highest)
    out_real = jnp.einsum("fbc,cdf->fbd", spec_real, cos_grid, precision=highest) - jnp.einsum(
        "fbc,cdf->fbd", spec_imag, sin_grid, precision=highest
    )
    out_imag = jnp.einsum("fbc,cdf->fbd", spec_real, sin_grid, precision=highest) + jnp.einsum(
        "fbc,cdf->fbd", spec_imag, cos_grid, precision=highest
    )
    result = jnp.einsum("fbd,fu->dbu", out_real, inverse_cos, precision=highest) + jnp.einsum(
        "fbd,fu->dbu", out_imag, inverse_sin, precision=highest
    )
    return result / math.sqrt(CHANS)


def solution(mesh):
    return jax.shard_map(
        shards,
        mesh=mesh,
        in_specs=(
            P(("groups", "section", "sub"), None, None),
            P(),
            P(("groups", "section", "sub"), None, None, None),
            P(),
            P(),
            P(),
        ),
        out_specs=P(None, ("groups", "section", "sub"), None),
        check_vma=False,
    )
```

profile of v0, /device:TPU:13, one launch (start us, length us, event | category | flops | bytes accessed | tf_op | source)
XLA Modules:
  0.0 1016.8 jit_solution(13702992276436314519)
XLA Ops:
  0.5 49.9 %reshape.190 = bf16[64,2,515,128]{3,2,1,0:T(8,128)(2,1)} reshape(bf16[64,2,65920]{2,1,0:T(2,128)(2,1)} %param.6) | data formatting | bytes 33751040 | tf_op jit(solution)/shard_map/reshape | solution.py:30
  50.4 7.8 fusion.31
  58.2 10.2 %fusion.30 = bf16[64,512,1024]{2,1,0:T(8,128)(2,1)} fusion(bf16[64,512,1024]{2,1,0:T(8,128)(2,1)} %fusion.31, bf16[64,2,515,128]{3,2,1,0:T(8,128)(2,1)} %reshape.190), kind=kLoop, calls=%fused_computation.41 | loop fusion | bytes 16777216
  68.5 10.2 %fusion.29 = bf16[64,512,1024]{2,1,0:T(8,128)(2,1)} fusion(bf16[64,512,1024]{2,1,0:T(8,128)(2,1)} %fusion.30, bf16[64,2,515,128]{3,2,1,0:T(8,128)(2,1)} %reshape.190), kind=kLoop, calls=%fused_computation.39 | loop fusion | bytes 16777216
  78.7 10.3 %fusion.28 = bf16[64,512,1024]{2,1,0:T(8,128)(2,1)} fusion(bf16[64,512,1024]{2,1,0:T(8,128)(2,1)} %fusion.29, bf16[64,2,515,128]{3,2,1,0:T(8,128)(2,1)} %reshape.190), kind=kLoop, calls=%fused_computation.37 | loop fusion | bytes 16777216
  89.0 7.9 fusion.27
  96.9 10.6 %fusion.26 = bf16[64,512,1024]{2,1,0:T(8,128)(2,1)} fusion(bf16[64,512,1024]{2,1,0:T(8,128)(2,1)} %fusion.27, bf16[64,2,515,128]{3,2,1,0:T(8,128)(2,1)} %reshape.190), kind=kLoop, calls=%fused_computation.33 | loop fusion | bytes 16777216
  107.5 10.2 %fusion.25 = bf16[64,512,1024]{2,1,0:T(8,128)(2,1)} fusion(bf16[64,512,1024]{2,1,0:T(8,128)(2,1)} %fusion.26, bf16[64,2,515,128]{3,2,1,0:T(8,128)(2,1)} %reshape.190), kind=kLoop, calls=%fused_computation.31 | loop fusion | bytes 16777216
  117.7 10.3 %fusion.24 = bf16[64,512,1024]{2,1,0:T(8,128)(2,1)} fusion(bf16[64,512,1024]{2,1,0:T(8,128)(2,1)} %fusion.25, bf16[64,2,515,128]{3,2,1,0:T(8,128)(2,1)} %reshape.190), kind=kLoop, calls=%fused_computation.29 | loop fusion | bytes 16777216 | tf_op jit(solution)/shard_map/concatenate | solution.py:31
  128.2 34.0 %fusion.14 = bf16[2,128,64,512]{3,1,2,0:T(8,128)(2,1)} fusion(bf16[64,512,1024]{2,1,0:T(8,128)(2,1)} %fusion.24, bf16[1,128,1024]{2,1,0:T(8,128)(2,1)S(1)} %get-tuple-element.10, bf16[1,128,1024]{2,1,0:T(8,128)(2,1)S(1)} %get-tuple-element.9), kind=kOutput, calls=%fused_computation.24 | convolution fusion | flops 17189306368 | bytes 84410368 | tf_op jit(solution)/shard_map/dot_general | solution.py:39
  162.3 18.5 %copy.81 = bf16[2,128,64,512]{3,2,0,1:T(8,128)(2,1)} copy(bf16[2,128,64,512]{3,1,2,0:T(8,128)(2,1)} %fusion.14) | data formatting | bytes 33554432 | tf_op jit(solution)/shard_map/convert_element_type | solution.py:42
  180.8 6.7 all-to-all-start
  187.4 0.6 pad_clamp_fusion
  188.0 4.5 gather_fusion
  192.6 4.3 scatter_custom_fusion
  197.5 352.0 %all-to-all-done = bf16[2,128,64,512]{3,2,0,1:T(8,128)(2,1)} async-done(((bf16[2,128,64,512]{3,2,0,1:T(8,128)(2,1)}), bf16[2,128,64,512]{3,2,0,1:T(8,128)(2,1)}, u32[]{:S(2)}, u32[]{:S(2)}) %all-to-all-start) | async-done | bytes 16777248 | tf_op jit(solution)/shard_map/all_to_all | solution.py:66
  549.6 8.7 copy.83
  558.3 39.3 %copy.84 = bf16[2,8,1024,512]{3,1,2,0:T(8,128)(2,1)} copy(bf16[2,8,1024,512]{3,2,1,0:T(8,128)(2,1)S(1)} %bitcast.159) | data formatting | bytes 33554432 | tf_op jit(solution)/shard_map/all_to_all | solution.py:66
  597.6 18.2 %gather_fusion.1 = bf16[1024,2,8,512]{3,2,1,0:T(8,128)(2,1)} fusion(bf16[2,8,1024,512]{3,1,2,0:T(8,128)(2,1)} %copy.84, s32[1024]{0:T(1024)S(1)} %fusion.112), kind=kCustom, calls=%fused_computation.1 | custom fusion | bytes 33558528 | tf_op jit(solution)/shard_map/jit(_take)/gather | solution.py:65
  615.9 14.9 %select_bitcast_fusion = bf16[2,8,1024,512]{3,1,0,2:T(8,128)(2,1)} fusion(bf16[1024,2,8,512]{3,2,1,0:T(8,128)(2,1)} %gather_fusion.1, pred[1024]{0:T(1024)(128)(4,1)S(1)} %compare_and_fusion), kind=kLoop, calls=%fused_computation.17 | loop fusion | flops 8388608 | bytes 33555456 | tf_op jit(solution)/shard_map/jit(_take)/select_n | solution.py:65
  630.8 23.2 %copy.86 = bf16[2,8,1024,512]{2,3,0,1:T(8,128)(2,1)} copy(bf16[2,8,1024,512]{3,1,0,2:T(8,128)(2,1)} %select_bitcast_fusion) | data formatting | bytes 33554432 | tf_op jit(solution)/shard_map/jit(_take)/select_n | solution.py:65
  654.0 32.2 %fusion.17 = f32[2,8,1024,512]{2,3,0,1:T(8,128)} fusion(bf16[2,8,1024,512]{2,3,0,1:T(8,128)(2,1)} %copy.86, bf16[8,2,1024,1024]{3,2,1,0:T(8,128)(2,1)} %param.8), kind=kOutput, calls=%fused_computation.25 | convolution fusion | flops 17179869184 | bytes 67108864 | tf_op jit(solution)/shard_map/cbi,pcit->pcbt/dot_general | solution.py:70
  686.2 32.5 %fusion.20 = f32[2,8,1024,512]{2,3,0,1:T(8,128)} fusion(bf16[2,8,1024,512]{2,3,0,1:T(8,128)(2,1)} %copy.86, bf16[8,2,1024,1024]{3,2,1,0:T(8,128)(2,1)} %param.8), kind=kOutput, calls=%fused_computation.26 | convolution fusion | flops 17179869184 | bytes 67108864 | tf_op jit(solution)/shard_map/cbi,pcit->pcbt/dot_general | solution.py:73
  718.7 29.5 %fusion.4 = f32[8,1024,512]{1,2,0:T(8,128)} fusion(f32[2,8,1024,512]{2,3,0,1:T(8,128)} %fusion.20, f32[2,8,1024,512]{2,3,0,1:T(8,128)} %fusion.17), kind=kLoop, calls=%fused_computation.10 | loop fusion | flops 20971520 | bytes 83886080 | tf_op jit(solution)/shard_map/add | solution.py:78
  748.2 17.5 %copy.89 = f32[8,1024,512]{2,0,1:T(8,128)} copy(f32[8,1024,512]{1,2,0:T(8,128)} %fusion.4) | data formatting | bytes 33554432 | tf_op jit(solution)/shard_map/add | solution.py:78
  765.7 18.2 %gather_fusion.2 = f32[1024,8,512]{2,1,0:T(8,128)} fusion(f32[8,1024,512]{2,0,1:T(8,128)} %copy.89, s32[1024]{0:T(1024)S(1)} %fusion.111), kind=kCustom, calls=%fused_computation.2 | custom fusion | bytes 33558528 | tf_op jit(solution)/shard_map/jit(_take)/gather | solution.py:79
  784.0 16.6 %copy.90 = f32[8,1024,512]{1,0,2:T(8,128)} copy(f32[8,1024,512]{2,0,1:T(8,128)} %bitcast.158) | data formatting | bytes 33554432 | tf_op jit(solution)/shard_map/jit(_take)/gather | solution.py:79
  800.6 10.8 %select_reduce_fusion = f32[8,1024,128]{1,0,2:T(8,128)} fusion(pred[1024]{0:T(1024)(128)(4,1)S(1)} %copy-done.5, f32[8,1024,512]{1,0,2:T(8,128)} %copy.90), kind=kLoop, calls=%fused_computation.21 | loop fusion | flops 7340032 | bytes 20972544 | tf_op jit(solution)/shard_map/reduce_sum | solution.py:47
  811.4 5.4 copy.91
  816.7 4.8 copy.92
  821.6 5.1 all-to-all-start.1
  826.8 0.9 gather_fusion.3
  828.0 6.5 fusion.10
  834.4 6.5 fusion.23
  841.0 7.2 fusion.135
  848.2 70.8 %all-to-all-done.1 = f32[8,16,64,128]{3,2,0,1:T(8,128)} async-done(((f32[8,16,64,128]{3,2,0,1:T(8,128)}), f32[8,16,64,128]{3,2,0,1:T(8,128)}, u32[]{:S(2)}, u32[]{:S(2)}) %all-to-all-start.1) | async-done | bytes 4194336 | tf_op jit(solution)/shard_map/all_to_all | solution.py:114
  919.0 3.4 bitcast_reduce_fusion
  922.4 4.0 fusion.48
  926.5 6.8 fusion.46
  933.3 6.7 fusion.49
  939.9 6.7 fusion.51
  946.6 10.2 %fusion.36 = f32[65,64,256]{2,1,0:T(8,128)} fusion(f32[128,256,65]{1,2,0:T(8,128)S(1)} %bitcast.157, f32[65,128,64]{1,0,2:T(8,128)S(1)} %fusion.49), kind=kOutput, calls=%fused_computation.49 | convolution fusion | flops 1635778560 | bytes 14909440 | tf_op jit(solution)/shard_map/fbc,cdf->fbd/dot_general | solution.py:122
  956.8 9.9 fusion.34
  966.7 9.4 fusion.55
  976.1 10.0 fusion.58
  986.1 9.8 fusion.42
  995.9 11.9 %multiply_bitcast_fusion = f32[256,64,128]{0,2,1:T(8,128)} fusion(f32[128,64,256]{2,0,1:T(8,128)S(1)} %fusion.42, f32[65,64,256]{2,1,0:T(8,128)S(1)} %fusion.55, f32[65]{0:T(128)S(1)} %fusion.115), kind=kOutput, calls=%fused_computation.44 | convolution fusion | flops 1640097664 | bytes 21037316 | tf_op jit(solution)/shard_map/fbd,fu->dbu/dot_general | solution.py:128
  1007.7 8.7 copy.111
  (50 shorter events, 1.8 us)
Async XLA Ops:
  0.0 188.0 %copy-start = (s32[1024]{0:T(1024)S(1)}, s32[1024]{0:T(1024)}, u32[]{:S(2)}) copy-start(s32[1024]{0:T(1024)} %param.9) | copy-start | bytes 12292
  117.7 10.4 %copy-start.6 = (f32[512]{0:T(512)S(1)}, f32[512]{0:T(512)}, u32[]{:S(2)}) copy-start(f32[512]{0:T(512)} %param.7) | copy-start | bytes 6148
  180.8 16.1 %copy-start.4 = (s32[1024]{0:T(1024)S(1)}, s32[1024]{0:T(1024)}, u32[]{:S(2)}) copy-start(s32[1024]{0:T(1024)} %param.10) | copy-start | bytes 12292
  180.8 368.8 %all-to-all-start = ((bf16[2,128,64,512]{3,2,0,1:T(8,128)(2,1)}), bf16[2,128,64,512]{3,2,0,1:T(8,128)(2,1)}, u32[]{:S(2)}, u32[]{:S(2)}) async-start(bf16[2,128,64,512]{3,2,0,1:T(8,128)(2,1)} %copy.81), calls=%async_computation | async-start | bytes 33554432 | tf_op jit(solution)/shard_map/all_to_all | solution.py:66
  784.0 16.6 %copy-start.5 = (pred[1024]{0:T(1024)(128)(4,1)S(1)}, pred[1024]{0:T(1024)(128)(4,1)}, u32[]{:S(2)}) copy-start(pred[1024]{0:T(1024)(128)(4,1)} %compare_and_fusion.1) | copy-start | bytes 3076
  816.7 9.9 copy-start.3
  821.6 97.4 %all-to-all-start.1 = ((f32[8,16,64,128]{3,2,0,1:T(8,128)}), f32[8,16,64,128]{3,2,0,1:T(8,128)}, u32[]{:S(2)}, u32[]{:S(2)}) async-start(f32[8,16,64,128]{3,2,0,1:T(8,128)} %copy.92), calls=%async_computation.1 | async-start | bytes 8388608 | tf_op jit(solution)/shard_map/all_to_all | solution.py:114
  926.4 20.1 %slice-start.3 = ((s8[9437184]{0:T(1024)(128)(4,1)}), s8[4194304]{0:T(1024)(128)(4,1)S(1)}, s32[]{:S(2)}) async-start(s8[9437184]{0:T(1024)(128)(4,1)} %bitcast.156), calls=%async_computation.5 | async-start | bytes 8388608
  926.5 20.1 %slice-start.4 = ((s8[9437184]{0:T(1024)(128)(4,1)}), s8[4194304]{0:T(1024)(128)(4,1)S(1)}, s32[]{:S(2)}) async-start(s8[9437184]{0:T(1024)(128)(4,1)} %bitcast.156), calls=%async_computation.6 | async-start | bytes 8388608
  933.2 13.4 %slice-start.5 = ((s8[9437184]{0:T(1024)(128)(4,1)}), s8[1048576]{0:T(1024)(128)(4,1)S(1)}, s32[]{:S(2)}) async-start(s8[9437184]{0:T(1024)(128)(4,1)} %bitcast.156), calls=%async_computation.7 | async-start | bytes 2097152
  946.6 20.1 %copy-start.2 = (f32[65,128,64]{1,0,2:T(8,128)}, f32[65,128,64]{1,0,2:T(8,128)S(1)}, u32[]{:S(2)}) copy-start(f32[65,128,64]{1,0,2:T(8,128)S(1)} %fusion.51) | copy-start | bytes 6389764
  946.6 20.1 %slice-start = ((s8[9437184]{0:T(1024)(128)(4,1)}), s8[4194304]{0:T(1024)(128)(4,1)S(1)}, s32[]{:S(2)}) async-start(s8[9437184]{0:T(1024)(128)(4,1)} %bitcast.154), calls=%async_computation.2 | async-start | bytes 8388608
  946.6 20.1 %slice-start.1 = ((s8[9437184]{0:T(1024)(128)(4,1)}), s8[4194304]{0:T(1024)(128)(4,1)S(1)}, s32[]{:S(2)}) async-start(s8[9437184]{0:T(1024)(128)(4,1)} %bitcast.154), calls=%async_computation.3 | async-start | bytes 8388608
  956.8 9.9 slice-start.2
  995.8 20.6 %copy-start.1 = (s32[1024]{0:T(1024)S(1)}, s32[1024]{0:T(1024)}, u32[]{:S(2)}) copy-start(s32[1024]{0:T(1024)} %param.9) | copy-start | bytes 12292
where the time goes:
time: 1030 us; the launch traced here: 1020 us
  waiting for transfers between devices  423 us (41%)
  local copies, waits for them, and re-layouts  324 us (31%)
  matrix products  186 us (18%)
  other arithmetic  71.4 us (7%)
  starting transfers between devices  11.8 us (1%)
    all_to_all x1, waiting for transfers between devices, shards(): lax.all_to_all(spectra_local, ('section', 'sub'), split_axis=1, concat_ax...  352 us
    all_to_all x1, waiting for transfers between devices, shards(): lax.all_to_all(outgoing, ('section', 'sub'), split_axis=1, concat_axis=0,...  70.8 us
    unnamed x34, local copies, waits for them, and re-layouts  67.5 us
    reshape x1, local copies, waits for them, and re-layouts, channelize(): frames = block_volts.reshape(input_count, 2, SPECTRA + TAPS - 1, CHANS)  49.9 us
    all_to_all x2, local copies, waits for them, and re-layouts, shards(): lax.all_to_all(spectra_local, ('section', 'sub'), split_axis=1, concat_ax...  48.1 us
    gather x2, local copies, waits for them, and re-layouts, shards(): power = jnp.take(power, beam_order, axis=1)  34.9 us
    dot_general x1, matrix products, channelize(): lax.dot_general(matrix, windows, (((2,), (2,)), ((), ())), preferred_elem...  34 us
    dot_general x1, matrix products, shards(): jnp.einsum('cbi,pcit->pcbt', weight_imag, ordered, preferred_element_type...  32.5 us
  transfers between devices with their start and end apart: 2, of which 2 were waited for; matrix products, arithmetic and copies ran while one was open for 3% of the time, Pallas kernels for 0%

commit v1 on v0

--- a/solution.py
+++ b/solution.py
@@ -3,6 +3,8 @@
 import jax
 import jax.numpy as jnp
 from jax import lax
+from jax.experimental import pallas as pl
+from jax.experimental.pallas import tpu as pltpu
 from jax.sharding import PartitionSpec as P
 
 CHANS = 128
@@ -12,6 +14,15 @@
 DOWN = 4
 SPECTRA = 512
 BINS = 128
+LANES = 128
+OWNER_AXES = ("section", "sub")
+VMEM_LIMIT = 56 << 20
+U_BLOCK = 16
+TRIAL_BLOCK = 16
+FREQS = BINS // 2 + 1
+FREQ_ROWS = 80
+FREQ_BLOCK = 5
+BEAM_BLOCK = 256
 
 
 def filter_matrix(prototype):
@@ -23,6 +34,371 @@
     real_rows = jnp.concatenate([cosine, sine_part], axis=1)
     imag_rows = jnp.concatenate([-sine_part, cosine], axis=1)
     return jnp.stack([real_rows, imag_rows], axis=0).astype(jnp.bfloat16)
+
+
+def channelize_kernel(owners, count, main_ref, *refs):
+    halo_refs = refs[: TAPS - 1]
+    bank_ref, out_ref, turned, spread = refs[TAPS - 1 :]
+    rows = owners * count
+    block = U_BLOCK * DOWN
+    half = main_ref.shape[0] // 2
+
+    def turn(step, carry):
+        start = pl.multiple_of(step * LANES, LANES)
+        turned[pl.ds(start, LANES), :] = main_ref[:, pl.ds(start, LANES)].T
+        return carry
+
+    lax.fori_loop(0, block, turn, 0, unroll=4)
+    for tap in range(TAPS - 1):
+        turned[(block + tap) * LANES : (block + tap + 1) * LANES, :] = halo_refs[tap][...].T
+    lane = lax.broadcasted_iota(jnp.int32, (rows, LANES), 1)
+    sign = jnp.where(lane < half, 1.0, -1.0).astype(jnp.float32)
+
+    def spectra(u, carry):
+        for pair in range(DOWN // 2):
+            base = u * DOWN + pair * 2
+            pieces = [
+                turned[pl.ds(pl.multiple_of((base + e) * LANES, LANES), TAPS * LANES), :]
+                for e in range(2)
+            ]
+            both = jnp.dot(
+                bank_ref[...],
+                jnp.concatenate(pieces, axis=1),
+                preferred_element_type=jnp.float32,
+            )
+            for e in range(2):
+                own = both[:rows, e * LANES : (e + 1) * LANES]
+                other = both[rows:, e * LANES : (e + 1) * LANES]
+                value = own + sign * pltpu.roll(other, half, axis=1)
+                m = pair * 2 + e
+                spread[pl.ds(m * U_BLOCK + u, rows, stride=block), :] = value
+        return carry
+
+    lax.fori_loop(0, U_BLOCK, spectra, 0, unroll=2)
+    out_ref[...] = spread[...].reshape(out_ref.shape).astype(jnp.bfloat16)
+
+
+def channelize_chunk(turned_volts, bank, owners, count):
+    width = turned_volts.shape[0]
+    block = U_BLOCK * DOWN
+    steps = SPECTRA // block
+    rows = owners * count
+    return pl.pallas_call(
+        lambda *refs: channelize_kernel(owners, count, *refs),
+        out_shape=jax.ShapeDtypeStruct((owners, count, DOWN, BINS, width), jnp.bfloat16),
+        grid=(steps,),
+        in_specs=[pl.BlockSpec((width, block * LANES), lambda g: (0, g))]
+        + [
+            pl.BlockSpec((width, LANES), lambda g, tap=tap: (0, (g + 1) * block + tap))
+            for tap in range(TAPS - 1)
+        ]
+        + [pl.BlockSpec((2 * rows, TAPS * LANES), lambda g: (0, 0))],
+        out_specs=pl.BlockSpec((owners, count, DOWN, U_BLOCK, width), lambda g: (0, 0, 0, g, 0)),
+        scratch_shapes=[
+            pltpu.VMEM(((block + TAPS - 1) * LANES, LANES), jnp.bfloat16),
+            pltpu.VMEM((rows * block, LANES), jnp.float32),
+        ],
+        compiler_params=pltpu.CompilerParams(vmem_limit_bytes=VMEM_LIMIT),
+        cost_estimate=pl.CostEstimate(
+            flops=2 * 2 * CHANS * width * SPECTRA * TAPS * LANES,
+            bytes_accessed=turned_volts.size * 2 + rows * SPECTRA * width * 2,
+            transcendentals=0,
+        ),
+        name="channelize",
+    )(turned_volts, *([turned_volts] * (TAPS - 1)), bank)
+
+
+def beam_kernel(sources, arrived_ref, weight_ref, pick_ref, out_ref, normed):
+    tile = pl.program_id(1)
+    inputs = weight_ref.shape[2]
+    part = inputs // sources
+    spectra = jnp.concatenate([arrived_ref[s, 0] for s in range(sources)], axis=1)
+    first = weight_ref[0, 0]
+    second = weight_ref[0, 1]
+    negative = -second
+    real_rows = []
+    imag_rows = []
+    for s in range(sources):
+        rows = slice(s * part, (s + 1) * part)
+        real_rows += [first[rows], negative[rows]]
+        imag_rows += [second[rows], first[rows]]
+    beam_real = jnp.dot(
+        spectra, jnp.concatenate(real_rows, axis=0), preferred_element_type=jnp.float32
+    )
+    beam_imag = jnp.dot(
+        spectra, jnp.concatenate(imag_rows, axis=0), preferred_element_type=jnp.float32
+    )
+    power = beam_real * beam_real + beam_imag * beam_imag
+    folded = power[:BINS]
+    for m in range(1, DOWN):
+        folded = folded + power[m * BINS : (m + 1) * BINS]
+    centred = folded - jnp.mean(folded, axis=0, keepdims=True)
+    spread = jnp.mean(centred * centred, axis=0, keepdims=True)
+    start = pl.multiple_of(tile * BEAM_BLOCK, BEAM_BLOCK)
+    normed[:, pl.ds(start, BEAM_BLOCK)] = (centred / jnp.sqrt(spread + 1e-06)).astype(jnp.bfloat16)
+
+    @pl.when(tile == pl.num_programs(1) - 1)
+    def _():
+        picked = lax.dot_general(
+            pick_ref[...],
+            normed[...],
+            (((1,), (1,)), ((), ())),
+            preferred_element_type=jnp.float32,
+        )
+        out_ref[...] = picked.astype(jnp.bfloat16).reshape(out_ref.shape)
+
+
+def beam_chunk(arrived, weights, pick, owners):
+    sources, count, spectra, width = arrived.shape
+    _, _, inputs, beams = weights.shape
+    return pl.pallas_call(
+        lambda *refs: beam_kernel(sources, *refs),
+        out_shape=jax.ShapeDtypeStruct((owners, count, beams // owners, BINS), jnp.bfloat16),
+        grid=(count, beams // BEAM_BLOCK),
+        in_specs=[
+            pl.BlockSpec((sources, 1, spectra, width), lambda c, b: (0, c, 0, 0)),
+            pl.BlockSpec((1, 2, inputs, BEAM_BLOCK), lambda c, b: (c, 0, 0, b)),
+            pl.BlockSpec((beams, beams), lambda c, b: (0, 0)),
+        ],
+        out_specs=pl.BlockSpec((owners, 1, beams // owners, BINS), lambda c, b: (0, c, 0, 0)),
+        scratch_shapes=[pltpu.VMEM((BINS, beams), jnp.bfloat16)],
+        compiler_params=pltpu.CompilerParams(vmem_limit_bytes=VMEM_LIMIT),
+        cost_estimate=pl.CostEstimate(
+            flops=count * 8 * spectra * inputs * beams,
+            bytes_accessed=arrived.size * 2 + weights.size * 2,
+            transcendentals=0,
+        ),
+        name="beamform",
+    )(arrived, weights, pick)
+
+
+def split_parts(values):
+    high = lax.reduce_precision(values, 8, 7)
+    return high.astype(jnp.bfloat16), (values - high).astype(jnp.bfloat16)
+
+
+def forward_table():
+    freq = jnp.arange(FREQ_ROWS, dtype=jnp.int32)
+    sample = jnp.arange(BINS, dtype=jnp.int32)
+    angles = (2.0 * math.pi / BINS) * (freq[:, None] * sample[None, :] % BINS).astype(jnp.float32)
+    used = (freq < FREQS)[:, None]
+    rows = jnp.concatenate(
+        [jnp.where(used, jnp.cos(angles), 0.0), jnp.where(used, -jnp.sin(angles), 0.0)], axis=0
+    )
+    return jnp.concatenate(split_parts(rows), axis=1)
+
+
+def inverse_table():
+    freq = jnp.arange(FREQ_ROWS, dtype=jnp.int32)
+    sample = jnp.arange(BINS, dtype=jnp.int32)
+    angles = (2.0 * math.pi / BINS) * (sample[:, None] * freq[None, :] % BINS).astype(jnp.float32)
+    edge = (freq == 0) | (freq == BINS // 2)
+    weight = jnp.where(freq < FREQS, jnp.where(edge, 1.0, 2.0), 0.0)
+    weight = weight / (BINS * math.sqrt(CHANS))
+    rows = jnp.concatenate([jnp.cos(angles) * weight, -jnp.sin(angles) * weight], axis=0)
+    high, low = split_parts(rows)
+    return jnp.concatenate([high, high, low], axis=1)
+
+
+def phase_table(delays):
+    freq = jnp.arange(FREQS, dtype=jnp.int32)
+    index = freq[:, None, None] * delays[None] % BINS
+    angles = (2.0 * math.pi / BINS) * index.astype(jnp.float32)
+    both = jnp.concatenate([jnp.cos(angles), jnp.sin(angles)], axis=2)
+    return jnp.concatenate(split_parts(both), axis=2)
+
+
+def split_inside(values):
+    high = values.astype(jnp.bfloat16)
+    return high, (values - high.astype(jnp.float32)).astype(jnp.bfloat16)
+
+
+def dedisperse_kernel(pieces, channels, trials, freq_steps, *refs):
+    series_refs = refs[:pieces]
+    phase_ref, forward_ref, inverse_ref, out_ref, spec, turned = refs[pieces:]
+    step = pl.program_id(0)
+    half = LANES // 2
+
+    def low_lanes(rows):
+        return lax.broadcasted_iota(jnp.int32, (rows, LANES), 1) < half
+
+    @pl.when(step == 0)
+    def _():
+        low = low_lanes(FREQ_ROWS)
+        tail = 16
+        for d in range(trials):
+            turned[(d + 1) * FREQ_ROWS - tail : (d + 1) * FREQ_ROWS, :] = jnp.zeros(
+                (tail, LANES), jnp.float32
+            )
+        base = 0
+        for ref in series_refs:
+            pairs = ref.shape[0]
+
+            def one_pair(pair, carry, ref=ref, base=base):
+                both = ref[pair]
+                result = lax.dot_general(
+                    forward_ref[...],
+                    jnp.concatenate([both, both], axis=1),
+                    (((1,), (1,)), ((), ())),
+                    preferred_element_type=jnp.float32,
+                )
+                real, imag = result[:FREQ_ROWS], result[FREQ_ROWS:]
+                even = jnp.where(low, real, pltpu.roll(imag, half, axis=1))
+                odd = jnp.where(low, pltpu.roll(real, half, axis=1), imag)
+                channel = base + 2 * pair
+                spec[pl.ds(channel, FREQ_ROWS, stride=channels), :] = even
+                spec[pl.ds(channel + 1, FREQ_ROWS, stride=channels), :] = odd
+                return carry
+
+            lax.fori_loop(0, pairs, one_pair, 0, unroll=2)
+            base += 2 * pairs
+
+    @pl.when(step < freq_steps)
+    def _():
+        sign = jnp.where(low_lanes(channels), -1.0, 1.0).astype(jnp.float32)
+        for local in range(FREQ_BLOCK):
+            freq = step * FREQ_BLOCK + local
+            own = spec[pl.ds(pl.multiple_of(freq * channels, channels), channels), :]
+            full = jnp.concatenate([own, sign * pltpu.roll(own, half, axis=1)], axis=0)
+            high, low = split_inside(full)
+            phase = phase_ref[local]
+            result = jnp.dot(
+                jnp.concatenate([phase, phase[:, : 2 * channels]], axis=1),
+                jnp.concatenate([high, high, low], axis=0),
+                preferred_element_type=jnp.float32,
+            )
+            turned[pl.ds(freq, trials, stride=FREQ_ROWS), :] = result
+
+    @pl.when(step >= freq_steps)
+    def _():
+        low_half = low_lanes(BINS)
+
+        def one_pair(pair, carry):
+            columns = []
+            for e in range(2):
+                trial = (step - freq_steps) * TRIAL_BLOCK + 2 * pair + e
+                start = pl.multiple_of(trial * FREQ_ROWS, FREQ_ROWS)
+                high, low = split_inside(turned[pl.ds(start, FREQ_ROWS), :])
+                columns.append(jnp.concatenate([high, low, high], axis=0))
+            result = jnp.dot(
+                inverse_ref[...],
+                jnp.concatenate(columns, axis=1),
+                preferred_element_type=jnp.float32,
+            )
+            first = result[:BINS, :LANES] + pltpu.roll(result[BINS:, :LANES], half, axis=1)
+            second = pltpu.roll(result[:BINS, LANES:], half, axis=1) + result[BINS:, LANES:]
+            both = jnp.where(low_half, first, second).T
+            out_ref[2 * pair] = both[:half]
+            out_ref[2 * pair + 1] = both[half:]
+            return carry
+
+        lax.fori_loop(0, TRIAL_BLOCK // 2, one_pair, 0, unroll=2)
+
+
+def dedisperse(series, phases, forward, inverse, beams):
+    freqs, trials, width = phases.shape
+    channels = width // 4
+    pieces = len(series)
+    freq_steps = freqs // FREQ_BLOCK
+    trial_steps = trials // TRIAL_BLOCK
+    series = [piece.reshape(-1, 2 * beams, BINS) for piece in series]
+    whole = [
+        pl.BlockSpec(piece.shape, lambda g: (0, 0, 0), pipeline_mode=pl.Buffered(1))
+        for piece in series
+    ]
+    return pl.pallas_call(
+        lambda *refs: dedisperse_kernel(pieces, channels, trials, freq_steps, *refs),
+        out_shape=jax.ShapeDtypeStruct((trials, beams, BINS), jnp.float32),
+        grid=(freq_steps + trial_steps,),
+        in_specs=whole
+        + [
+            pl.BlockSpec(
+                (FREQ_BLOCK, trials, width),
+                lambda g: (jnp.minimum(g, freq_steps - 1), 0, 0),
+            ),
+            pl.BlockSpec(forward.shape, lambda g: (0, 0)),
+            pl.BlockSpec(inverse.shape, lambda g: (0, 0)),
+        ],
+        out_specs=pl.BlockSpec(
+            (TRIAL_BLOCK, beams, BINS), lambda g: (jnp.maximum(g - freq_steps, 0), 0, 0)
+        ),
+        scratch_shapes=[
+            pltpu.VMEM((FREQ_ROWS * channels, LANES), jnp.float32),
+            pltpu.VMEM((trials * FREQ_ROWS, LANES), jnp.float32),
+        ],
+        compiler_params=pltpu.CompilerParams(vmem_limit_bytes=VMEM_LIMIT),
+        cost_estimate=pl.CostEstimate(
+            flops=freqs * trials * 6 * channels * LANES * 2 * 4,
+            bytes_accessed=phases.size * 2 + trials * beams * BINS * 4,
+            transcendentals=0,
+        ),
+        name="dedisperse",
+    )(*series, phases, forward, inverse)
+
+
+def shards_wide(voltages, prototype, beam_weights, input_order, beam_order, trial_delays):
+    owners = lax.axis_size("section") * lax.axis_size("sub")
+    chan_dev, _, beams, inputs = beam_weights.shape
+    local_inputs = voltages.shape[0]
+    trials = trial_delays.shape[0]
+    cuts = sorted({0, chan_dev // 8, chan_dev // 2, chan_dev})
+    parts = list(zip(cuts[:-1], cuts[1:]))
+
+    turned_volts = jnp.transpose(voltages, (1, 0, 2)).reshape(2 * local_inputs, -1)
+    bank = filter_matrix(prototype)[0].reshape(owners, chan_dev, 2, TAPS * LANES)
+    bank = jnp.transpose(bank, (2, 0, 1, 3))
+    input_pick = (
+        input_order[:, None] == jnp.arange(inputs, dtype=jnp.int32)[None, :]
+    ).astype(jnp.bfloat16)
+    beam_pick = (
+        beam_order[:, None] == jnp.arange(beams, dtype=jnp.int32)[None, :]
+    ).astype(jnp.bfloat16)
+    delays = trial_delays.reshape(trials, owners, chan_dev)
+
+    def exchange(piece):
+        return lax.all_to_all(piece, OWNER_AXES, split_axis=0, concat_axis=0, tiled=True)
+
+    def spectra_of(low, high):
+        rows = bank[:, :, low:high].reshape(-1, TAPS * LANES)
+        return channelize_chunk(turned_volts, rows, owners, high - low)
+
+    def weights_of(low, high):
+        return jnp.einsum(
+            "ip,cqbp->cqib",
+            input_pick,
+            beam_weights[low:high],
+            preferred_element_type=jnp.float32,
+        ).astype(jnp.bfloat16)
+
+    def beams_of(arrived, weights):
+        spectra = arrived.reshape(owners, -1, SPECTRA, 2 * local_inputs)
+        return beam_chunk(spectra, weights, beam_pick, owners)
+
+    split = parts[-1][0]
+    delays = jnp.concatenate(
+        [delays[:, :, :split].reshape(trials, -1), delays[:, :, split:].reshape(trials, -1)], axis=1
+    )
+    phases = phase_table(delays)
+
+    arrived, weights, outgoing = [], [], []
+    for step, (low, high) in enumerate(parts):
+        piece = spectra_of(low, high)
+        if step >= 2:
+            outgoing.append(beams_of(arrived[step - 2], weights[step - 2]))
+            outgoing[-1], piece = lax.optimization_barrier((outgoing[-1], piece))
+        if step == len(parts) - 1:
+            phases, piece = lax.optimization_barrier((phases, piece))
+        weights.append(weights_of(low, high))
+        arrived.append(exchange(piece))
+    if len(parts) >= 2:
+        outgoing.append(beams_of(arrived[-2], weights[-2]))
+        early = outgoing[0] if len(outgoing) == 1 else jnp.concatenate(outgoing, axis=1)
+        early, weights[-1], arrived[-1] = lax.optimization_barrier((early, weights[-1], arrived[-1]))
+        series = [exchange(early)]
+    else:
+        series = []
+    series.append(exchange(beams_of(arrived[-1], weights[-1])))
+    return dedisperse(series, phases, forward_table(), inverse_table(), beams // owners)
 
 
 def channelize(block_volts, matrix):
@@ -47,7 +423,7 @@
     return series.reshape(shape_head + (series.shape[-1] // DOWN, DOWN)).sum(axis=-1)
 
 
-def shards(voltages, prototype, beam_weights, input_order, beam_order, trial_delays):
+def shards_narrow(voltages, prototype, beam_weights, input_order, beam_order, trial_delays):
     section_count = lax.axis_size("section")
     sub_count = lax.axis_size("sub")
     owners = section_count * sub_count
@@ -132,8 +508,11 @@
 
 
 def solution(mesh):
+    owners = mesh.shape["section"] * mesh.shape["sub"]
+    wide = 2 * (INPUTS // owners) == LANES
+
     return jax.shard_map(
-        shards,
+        shards_wide if wide else shards_narrow,
         mesh=mesh,
         in_specs=(
             P(("groups", "section", "sub"), None, None),

time: 1030 us -> 591 us (0.57); the launches traced: 1020 us -> 590 us
  local copies, waits for them, and re-layouts: 324 us -> 19 us
  waiting for transfers between devices: 423 us -> 159 us
  Pallas kernels: 0 us -> 256 us
  matrix products: 186 us -> 53 us
  blocking collectives: 0 us -> 29.7 us
  other arithmetic: 71.4 us -> 50.7 us
  starting transfers between devices: 11.8 us -> 22.4 us
    all_to_all x2 -> x4, waiting for transfers between devices: 423 us -> 159 us  [exchange(): lax.all_to_all(piece, OWNER_AXES, split_axis=0, concat_axis=0, tiled=True)]
    pallas_call x0 -> x7, Pallas kernels: none -> 256 us  [the longest x3 138 us: channelize_chunk(): pl.pallas_call(lambda *refs: channelize_kernel(owners, count, *refs), out...]
    dot_general x13 -> x3, matrix products: 186 us -> 53 us  [weights_of(): jnp.einsum('ip,cqbp->cqib', input_pick, beam_weights[low:high], preferred...]
    unnamed x34 -> x13, local copies, waits for them, and re-layouts: 67.5 us -> 1.08 us
    gather x5 -> x0, local copies, waits for them, and re-layouts: 58.5 us -> none  [the longest x2 34.9 us: shards(): power = jnp.take(power, beam_order, axis=1)]
    reshape x2 -> x4, local copies, waits for them, and re-layouts: 54.7 us -> 1.45 us  [the longest x2 1.4 us: spectra_of(): rows = bank[:, :, low:high].reshape(-1, TAPS * LANES)]
    all_to_all x2 -> x0, local copies, waits for them, and re-layouts: 48.1 us -> none  [shards(): lax.all_to_all(spectra_local, ('section', 'sub'), split_axis=1, concat_ax...]
    cos x0 -> x1, other arithmetic: none -> 32.4 us  [phase_table(): both = jnp.concatenate([jnp.cos(angles), jnp.sin(angles)], axis=2)]
  transfers between devices with their start and end apart: 2 -> 4, of which waited for: 2 -> 3; matrix products, arithmetic and copies ran while one was open for 3% -> 18% of each run, Pallas kernels for 0% -> 22%
where the time goes in v1:
time: 591 us; the launch traced here: 590 us
  Pallas kernels  256 us (43%)
  waiting for transfers between devices  159 us (27%)
  matrix products  53 us (9%)
  other arithmetic  50.7 us (9%)
  blocking collectives  29.7 us (5%)
  starting transfers between devices  22.4 us (4%)
  local copies, waits for them, and re-layouts  19 us (3%)
    all_to_all x4, waiting for transfers between devices, exchange(): lax.all_to_all(piece, OWNER_AXES, split_axis=0, concat_axis=0, tiled=True)  159 us
    pallas_call x3, Pallas kernels, channelize_chunk(): pl.pallas_call(lambda *refs: channelize_kernel(owners, count, *refs), out...  138 us
    pallas_call x1, Pallas kernels, dedisperse(): pl.pallas_call(lambda *refs: dedisperse_kernel(pieces, channels, trials,...  59.1 us
    pallas_call x3, Pallas kernels, beam_chunk(): pl.pallas_call(lambda *refs: beam_kernel(sources, *refs), out_shape=jax.S...  58.9 us
    dot_general x3, matrix products, weights_of(): jnp.einsum('ip,cqbp->cqib', input_pick, beam_weights[low:high], preferred...  53 us
    cos x1, other arithmetic, phase_table(): both = jnp.concatenate([jnp.cos(angles), jnp.sin(angles)], axis=2)  32.4 us
    all_to_all x1, blocking collectives, exchange(): lax.all_to_all(piece, OWNER_AXES, split_axis=0, concat_axis=0, tiled=True)  29.7 us
    all_to_all x4, starting transfers between devices, exchange(): lax.all_to_all(piece, OWNER_AXES, split_axis=0, concat_axis=0, tiled=True)  22.4 us
  transfers between devices with their start and end apart: 4, of which 3 were waited for; matrix products, arithmetic and copies ran while one was open for 18% of the time, Pallas kernels for 22%

profile of v1, /device:TPU:13, one launch (start us, length us, event | category | flops | bytes accessed | tf_op | source)
XLA Modules:
  0.0 589.6 jit_solution(16072656932305394713)
XLA Ops:
  0.0 0.3 fusion.56
  0.3 0.3 fusion.55
  0.6 0.7 fusion.34
  1.4 0.2 reshape_squeeze.3
  1.6 0.6 copy.9
  2.2 15.2 %copy.8 = bf16[2,64,65920]{2,1,0:T(8,128)(2,1)} copy(bf16[2,64,65920]{2,0,1:T(2,128)(2,1)} %bitcast.62) | data formatting | bytes 33751040 | tf_op jit(solution)/shard_map/transpose | solution.py:347
  17.4 40.2 %channelize.3 = bf16[16,1,4,128,128]{4,3,2,1,0:T(8,128)(2,1)} custom-call(bf16[128,65920]{1,0:T(8,128)(2,1)} %bitcast.50, bf16[128,65920]{1,0:T(8,128)(2,1)} %bitcast.51, bf16[128,65920]{1,0:T(8,128)(2,1)} %bitcast.52, bf16[128,65920]{1,0:T(8,128)(2,1)} %bitcast.53, bf16[32,512]{1,0:T(8,128)(2,1)} %bitcast.72), custom_call_target="tpu_custom_call" | custom-call | flops 17179869184 | bytes 18972672 | tf_op jit(solution)/shard_map/channelize/pallas_call | solution.py:86
  57.6 6.5 %all-to-all-start = ((bf16[16,1,4,128,128]{4,3,2,1,0:T(8,128)(2,1)}), bf16[16,1,4,128,128]{4,3,2,1,0:T(8,128)(2,1)S(1)}, u32[]{:S(2)}, u32[]{:S(2)}) async-start(bf16[16,1,4,128,128]{4,3,2,1,0:T(8,128)(2,1)} %channelize.3), calls=%async_computation | async-start | bytes 4194304 | tf_op jit(solution)/shard_map/all_to_all | solution.py:359
  64.2 0.1 slice.35
  64.2 0.1 copy.11
  64.3 0.7 reshape.111.refs_4_
  65.0 46.5 %channelize.5 = bf16[16,3,4,128,128]{4,3,2,1,0:T(8,128)(2,1)} custom-call(bf16[128,65920]{1,0:T(8,128)(2,1)} %bitcast.54, bf16[128,65920]{1,0:T(8,128)(2,1)} %bitcast.55, bf16[128,65920]{1,0:T(8,128)(2,1)} %bitcast.56, bf16[128,65920]{1,0:T(8,128)(2,1)} %bitcast.57, bf16[96,512]{1,0:T(8,128)(2,1)} %reshape.111.refs_4_), custom_call_target="tpu_custom_call" | custom-call | flops 17179869184 | bytes 23166976 | tf_op jit(solution)/shard_map/channelize/pallas_call | solution.py:86
  111.6 0.0 all-to-all-done
  111.6 6.2 %all-to-all-start.1 = ((bf16[16,3,4,128,128]{4,3,2,1,0:T(8,128)(2,1)}), bf16[16,3,4,128,128]{4,3,2,1,0:T(8,128)(2,1)}, u32[]{:S(2)}, u32[]{:S(2)}) async-start(bf16[16,3,4,128,128]{4,3,2,1,0:T(8,128)(2,1)} %channelize.5), calls=%async_computation.1 | async-start | bytes 12582912 | tf_op jit(solution)/shard_map/all_to_all | solution.py:359
  117.7 0.1 slice.34
  117.8 0.1 copy.10
  117.9 0.7 reshape.110.refs_4_
  118.6 0.0 copy-done.3
  118.6 0.1 copy.12
  118.8 0.1 copy.13
  118.9 0.0 copy-done.4
  118.9 1.8 fusion.25.refs_2_
  120.7 32.4 %fusion.16 = (f32[65,256,128]{2,1,0:T(8,128)S(1)}, f32[65,256,128]{2,1,0:T(8,128)S(1)}) fusion(s32[256,128]{1,0:T(8,128)S(1)} %copy.13), kind=kLoop, calls=%fused_computation.21 | loop fusion | flops 29818880 | bytes 17170432 | tf_op jit(solution)/shard_map/cos | solution.py:207
  153.1 0.0 copy-done
  153.1 4.4 reduce-precision_convert_fusion
  157.5 0.0 copy-start.5
  157.5 6.7 %pad_maximum_fusion.1.refs_2_ = bf16[65,256,512]{2,1,0:T(8,128)(2,1)} fusion(bf16[65,256,256]{2,1,0:T(8,128)(2,1)S(1)} %get-tuple-element.20, bf16[65,256,256]{2,1,0:T(8,128)(2,1)S(1)} %get-tuple-element.19), kind=kLoop, calls=%fused_computation.4 | loop fusion | flops 34078720 | bytes 34078720 | tf_op jit(solution)/shard_map/concatenate | solution.py:208
  164.2 0.0 copy-done.5
  164.2 8.4 %convert_bitcast_fusion.2.refs_1_ = bf16[1,2,1024,1024]{3,2,1,0:T(8,128)(2,1)} fusion(bf16[8,2,1024,1024]{3,2,1,0:T(8,128)(2,1)} %param.8, s32[1024]{0:T(1024)S(1)} %copy-done.5), kind=kOutput, calls=%fused_computation.25 | convolution fusion | flops 4298113024 | bytes 8392704 | tf_op jit(solution)/shard_map/ip,cqbp->cqib/dot_general | solution.py:366
  172.6 51.0 %channelize.4 = bf16[16,4,4,128,128]{4,3,2,1,0:T(8,128)(2,1)} custom-call(bf16[128,65920]{1,0:T(8,128)(2,1)} %bitcast.58, bf16[128,65920]{1,0:T(8,128)(2,1)} %bitcast.59, bf16[128,65920]{1,0:T(8,128)(2,1)} %bitcast.60, bf16[128,65920]{1,0:T(8,128)(2,1)} %bitcast.61, bf16[128,512]{1,0:T(8,128)(2,1)} %reshape.110.refs_4_), custom_call_target="tpu_custom_call" | custom-call | flops 17179869184 | bytes 25264128 | tf_op jit(solution)/shard_map/channelize/pallas_call | solution.py:86
  223.6 9.3 %beamform.3 = bf16[16,1,64,128]{3,2,1,0:T(8,128)(2,1)} custom-call(bf16[16,1,512,128]{3,2,1,0:T(8,128)(2,1)} %bitcast.63, bf16[1,2,1024,1024]{3,2,1,0:T(8,128)(2,1)} %convert_bitcast_fusion.2.refs_1_, bf16[1024,1024]{1,0:T(8,128)(2,1)} %fusion.25.refs_2_), custom_call_target="tpu_custom_call" | custom-call | flops 4294967296 | bytes 6291456 | tf_op jit(solution)/shard_map/beamform/pallas_call | solution.py:154
  232.9 22.3 %all-to-all-done.1 = bf16[16,3,4,128,128]{4,3,2,1,0:T(8,128)(2,1)} async-done(((bf16[16,3,4,128,128]{4,3,2,1,0:T(8,128)(2,1)}), bf16[16,3,4,128,128]{4,3,2,1,0:T(8,128)(2,1)}, u32[]{:S(2)}, u32[]{:S(2)}) %all-to-all-start.1) | async-done | bytes 6291488 | tf_op jit(solution)/shard_map/all_to_all | solution.py:359
  255.2 4.8 all-to-all-start.2
  259.9 20.4 %convert_bitcast_fusion.1.refs_1_ = bf16[3,2,1024,1024]{3,2,1,0:T(8,128)(2,1)} fusion(bf16[8,2,1024,1024]{3,2,1,0:T(8,128)(2,1)} %param.8, s32[1024]{0:T(1024)S(1)} %copy-done.5), kind=kOutput, calls=%fused_computation.11 | convolution fusion | flops 12892241920 | bytes 25169920 | tf_op jit(solution)/shard_map/ip,cqbp->cqib/dot_general | solution.py:366
  280.3 24.2 %convert_bitcast_fusion.refs_1_ = bf16[4,2,1024,1024]{3,2,1,0:T(8,128)(2,1)} fusion(bf16[8,2,1024,1024]{3,2,1,0:T(8,128)(2,1)} %param.8, s32[1024]{0:T(1024)S(1)} %copy-done.5), kind=kOutput, calls=%fused_computation.5 | convolution fusion | flops 17189306368 | bytes 33558528 | tf_op jit(solution)/shard_map/ip,cqbp->cqib/dot_general | solution.py:366
  304.5 21.8 %beamform.4 = bf16[16,3,64,128]{3,2,1,0:T(8,128)(2,1)} custom-call(bf16[16,3,512,128]{3,2,1,0:T(8,128)(2,1)} %bitcast.10.refs_0_, bf16[3,2,1024,1024]{3,2,1,0:T(8,128)(2,1)} %convert_bitcast_fusion.1.refs_1_, bf16[1024,1024]{1,0:T(8,128)(2,1)} %fusion.25.refs_2_), custom_call_target="tpu_custom_call" | custom-call | flops 12884901888 | bytes 18874368 | tf_op jit(solution)/shard_map/beamform/pallas_call | solution.py:154
  326.3 2.2 pad_maximum_fusion.2
  328.5 113.8 %all-to-all-done.2 = bf16[16,4,4,128,128]{4,3,2,1,0:T(8,128)(2,1)} async-done(((bf16[16,4,4,128,128]{4,3,2,1,0:T(8,128)(2,1)}), bf16[16,4,4,128,128]{4,3,2,1,0:T(8,128)(2,1)}, u32[]{:S(2)}, u32[]{:S(2)}) %all-to-all-start.2) | async-done | bytes 8388640 | tf_op jit(solution)/shard_map/all_to_all | solution.py:359
  442.3 27.9 %beamform.5 = bf16[16,4,64,128]{3,2,1,0:T(8,128)(2,1)} custom-call(bf16[16,4,512,128]{3,2,1,0:T(8,128)(2,1)} %bitcast.18.refs_0_, bf16[4,2,1024,1024]{3,2,1,0:T(8,128)(2,1)} %convert_bitcast_fusion.refs_1_, bf16[1024,1024]{1,0:T(8,128)(2,1)} %fusion.25.refs_2_), custom_call_target="tpu_custom_call" | custom-call | flops 17179869184 | bytes 25165824 | tf_op jit(solution)/shard_map/beamform/pallas_call | solution.py:154
  470.1 29.7 %all_to_all.25 = bf16[16,4,64,128]{3,2,1,0:T(8,128)(2,1)} all-to-all(bf16[16,4,64,128]{3,2,1,0:T(8,128)(2,1)} %beamform.5), channel_id=1, replica_groups=mesh['groups'=2,'section'=8,'sub'=2] {'section','sub'}, dimensions={0} | all-to-all | bytes 2097152 | tf_op jit(solution)/shard_map/all_to_all | solution.py:359
  499.8 4.9 all-to-all-start.3
  504.8 0.2 cosine_select_fusion
  505.0 0.6 pad_maximum_fusion.7.refs_3_
  505.6 0.3 cosine_multiply_fusion
  505.9 0.8 pad_maximum_fusion.5.refs_4_
  506.7 22.9 %all-to-all-done.3 = bf16[16,4,64,128]{3,2,1,0:T(8,128)(2,1)S(1)} async-done(((bf16[16,4,64,128]{3,2,1,0:T(8,128)(2,1)}), bf16[16,4,64,128]{3,2,1,0:T(8,128)(2,1)S(1)}, u32[]{:S(2)}, u32[]{:S(2)}) %all-to-all-start.3) | async-done | bytes 1048608 | tf_op jit(solution)/shard_map/all_to_all | solution.py:359
  529.6 1.0 copy-done.1
  530.6 59.1 %dedisperse.1 = f32[256,64,128]{2,1,0:T(8,128)} custom-call(bf16[32,128,128]{2,1,0:T(8,128)(2,1)} %bitcast.67, bf16[32,128,128]{2,1,0:T(8,128)(2,1)} %bitcast.66, bf16[65,256,512]{2,1,0:T(8,128)(2,1)} %pad_maximum_fusion.1.refs_2_, bf16[160,256]{1,0:T(8,128)(2,1)} %pad_maximum_fusion.7.refs_3_, bf16[256,240]{1,0:T(8,128)(2,1)} %pad_maximum_fusion.5.refs_4_), custom_call_target="tpu_custom_call" | custom-call | flops 13086228480 | bytes 25427968 | tf_op jit(solution)/shard_map/dedisperse/pallas_call | solution.py:309
  (18 shorter events, 0.3 us)
Async XLA Ops:
  57.6 53.9 %all-to-all-start = ((bf16[16,1,4,128,128]{4,3,2,1,0:T(8,128)(2,1)}), bf16[16,1,4,128,128]{4,3,2,1,0:T(8,128)(2,1)S(1)}, u32[]{:S(2)}, u32[]{:S(2)}) async-start(bf16[16,1,4,128,128]{4,3,2,1,0:T(8,128)(2,1)} %channelize.3), calls=%async_computation | async-start | bytes 4194304 | tf_op jit(solution)/shard_map/all_to_all | solution.py:359
  111.6 7.0 %copy-start.3 = (s32[256,128]{1,0:T(8,128)S(1)}, s32[256,128]{1,0:T(8,128)}, u32[]{:S(2)}) copy-start(s32[256,128]{1,0:T(8,128)} %param.11) | copy-start | bytes 393220
  111.6 7.3 %copy-start.4 = (s32[1024]{0:T(1024)S(1)}, s32[1024]{0:T(1024)}, u32[]{:S(2)}) copy-start(s32[1024]{0:T(1024)} %param.10) | copy-start | bytes 12292
  111.6 41.5 %copy-start = (bf16[16,1,4,128,128]{4,3,2,1,0:T(8,128)(2,1)}, bf16[16,1,4,128,128]{4,3,2,1,0:T(8,128)(2,1)S(1)}, u32[]{:S(2)}) copy-start(bf16[16,1,4,128,128]{4,3,2,1,0:T(8,128)(2,1)S(1)} %all-to-all-done) | copy-start | bytes 6291460
  111.6 143.6 %all-to-all-start.1 = ((bf16[16,3,4,128,128]{4,3,2,1,0:T(8,128)(2,1)}), bf16[16,3,4,128,128]{4,3,2,1,0:T(8,128)(2,1)}, u32[]{:S(2)}, u32[]{:S(2)}) async-start(bf16[16,3,4,128,128]{4,3,2,1,0:T(8,128)(2,1)} %channelize.5), calls=%async_computation.1 | async-start | bytes 12582912 | tf_op jit(solution)/shard_map/all_to_all | solution.py:359
  157.5 6.7 %copy-start.5 = (s32[1024]{0:T(1024)S(1)}, s32[1024]{0:T(1024)}, u32[]{:S(2)}) copy-start(s32[1024]{0:T(1024)} %param.9) | copy-start | bytes 12292
  255.2 187.1 %all-to-all-start.2 = ((bf16[16,4,4,128,128]{4,3,2,1,0:T(8,128)(2,1)}), bf16[16,4,4,128,128]{4,3,2,1,0:T(8,128)(2,1)}, u32[]{:S(2)}, u32[]{:S(2)}) async-start(bf16[16,4,4,128,128]{4,3,2,1,0:T(8,128)(2,1)} %channelize.4), calls=%async_computation.2 | async-start | bytes 16777216 | tf_op jit(solution)/shard_map/all_to_all | solution.py:359
  304.5 21.8 %copy-start.2 = (bf16[16,1,64,128]{3,2,1,0:T(8,128)(2,1)S(1)}, bf16[16,1,64,128]{3,2,1,0:T(8,128)(2,1)}, u32[]{:S(2)}) copy-start(bf16[16,1,64,128]{3,2,1,0:T(8,128)(2,1)} %beamform.3) | copy-start | bytes 786436
  499.8 29.8 %all-to-all-start.3 = ((bf16[16,4,64,128]{3,2,1,0:T(8,128)(2,1)}), bf16[16,4,64,128]{3,2,1,0:T(8,128)(2,1)S(1)}, u32[]{:S(2)}, u32[]{:S(2)}) async-start(bf16[16,4,64,128]{3,2,1,0:T(8,128)(2,1)} %pad_maximum_fusion.2), calls=%async_computation.3 | async-start | bytes 2097152 | tf_op jit(solution)/shard_map/all_to_all | solution.py:359
  529.6 1.0 copy-start.1
